TPU v7x, 256 devices: a whole 4x4x8 slice. The times are simulated.
256 devices in a mesh: ta: 8 (over y_hi, x), xyz: 32 (over z, y_lo, core).
Axes of the slice: x: 4, y: 4 (y_hi: 2, y_lo: 2; y = y_hi * 2 + y_lo), z: 8, core: 2. Of those that a mesh axis runs over, the one named last changes fastest.
Arguments:
- gauge: float32 [4, 2, 3, 3, 16, 32, 1, 512], P(None, None, None, None, 'ta', 'xyz'), may hold values from -2.4 to 2.4
- clover_inverse: bfloat16 [2, 2, 6, 6, 16, 32, 1, 512], P(None, None, None, None, 'ta', 'xyz'), may hold values from -0.61 to 1
- source: float32 [2, 4, 3, 16, 32, 1, 512], P(None, None, None, 'ta', 'xyz'), may hold values from -6 to 6
- xi: float32 [2, 4, 3, 16, 32, 1, 512], P(None, None, None, 'ta', 'xyz'), may hold values from -6 to 6
- eta: float32 [2, 4, 3, 16, 32, 1, 512], P(None, None, None, 'ta', 'xyz'), may hold values from -6 to 6
- momentum: float32 [4, 2, 3, 3, 16, 32, 1, 512], P(None, None, None, None, 'ta', 'xyz'), may hold values from -6 to 6
Outputs:
- solution: float32 [2, 4, 3, 16, 32, 1, 512], P(None, None, None, 'ta', 'xyz')
- new_momentum: float32 [4, 2, 3, 3, 16, 32, 1, 512], P(None, None, None, None, 'ta', 'xyz')
All inputs are finite; a program needn't handle non-finite values.
Results may differ from a plain program's by a relative error of at most 0.022.
Values may be sent and summed in bfloat16 or wider, within the bound.
A program may use at most 64 MiB of HBM per device.

v0:
```python
import functools

import jax
import jax.numpy as jnp
from jax import lax
from jax.experimental import pallas as pl
from jax.experimental.pallas import tpu as pltpu
from jax.sharding import PartitionSpec as P

NZ = 64
ITERS = 8

hop_scale = 0.18
step_size = 0.25

ROWS = 8
LANES = 128
SLICE = 4


def combine(base, sign, term):
    return base + term if sign > 0 else base - term


def rotated(direction, sign, real, imag):
    if direction == 0:
        return [(sign, real[0]), (sign, real[1])], [(sign, imag[0]), (sign, imag[1])]
    if direction == 1:
        sig_real = [(1, real[1]), (1, real[0])]
        sig_imag = [(1, imag[1]), (1, imag[0])]
    elif direction == 2:
        sig_real = [(1, imag[1]), (-1, imag[0])]
        sig_imag = [(-1, real[1]), (1, real[0])]
    else:
        sig_real = [(1, real[0]), (-1, real[1])]
        sig_imag = [(1, imag[0]), (-1, imag[1])]
    return [(-sign * s, v) for s, v in sig_imag], [(sign * s, v) for s, v in sig_real]


def project(direction, sign, spinor):
    inverse_sign = sign if direction == 0 else -sign
    lower_real, lower_imag = rotated(
        direction, inverse_sign, [spinor[0, 2], spinor[0, 3]], [spinor[1, 2], spinor[1, 3]]
    )
    real = [combine(spinor[0, s], *lower_real[s]) for s in range(2)]
    imag = [combine(spinor[1, s], *lower_imag[s]) for s in range(2)]
    return real, imag


def add_expanded(total, direction, sign, half):
    real, imag = half
    lower_real, lower_imag = rotated(direction, sign, real, imag)
    new_real = [total[0][s] + real[s] for s in range(2)]
    new_real += [combine(total[0][2 + s], *lower_real[s]) for s in range(2)]
    new_imag = [total[1][s] + imag[s] for s in range(2)]
    new_imag += [combine(total[1][2 + s], *lower_imag[s]) for s in range(2)]
    return [new_real, new_imag]


def link_apply(links, direction, half):
    real, imag = half
    out_real, out_imag = [None, None], [None, None]
    for b in range(3):
        mat_real = links[direction, 0, :, b]
        mat_imag = links[direction, 1, :, b]
        for s in range(2):
            vec_real, vec_imag = real[s][b : b + 1], imag[s][b : b + 1]
            part_real = mat_real * vec_real - mat_imag * vec_imag
            part_imag = mat_real * vec_imag + mat_imag * vec_real
            out_real[s] = part_real if b == 0 else out_real[s] + part_real
            out_imag[s] = part_imag if b == 0 else out_imag[s] + part_imag
    return out_real, out_imag


def dagger_apply(links, direction, half):
    real, imag = half
    out_real, out_imag = [None, None], [None, None]
    for b in range(3):
        mat_real = links[direction, 0, b]
        mat_imag = links[direction, 1, b]
        for s in range(2):
            vec_real, vec_imag = real[s][b : b + 1], imag[s][b : b + 1]
            part_real = mat_real * vec_real + mat_imag * vec_imag
            part_imag = mat_real * vec_imag - mat_imag * vec_real
            out_real[s] = part_real if b == 0 else out_real[s] + part_real
            out_imag[s] = part_imag if b == 0 else out_imag[s] + part_imag
    return out_real, out_imag


def row_of(shape):
    return lax.broadcasted_iota(jnp.int32, shape, len(shape) - 2)


def lane_of(shape):
    return lax.broadcasted_iota(jnp.int32, shape, len(shape) - 1)


def roll(x, shift, axis):
    return pltpu.roll(x, shift, axis=x.ndim - 2 + axis)


def swap_slices(x):
    return roll(x, SLICE, 0)


def ahead_of(direction, x):
    if direction == 3:
        last = lane_of(x.shape) % NZ == NZ - 1
        return jnp.where(last, roll(x, NZ - 1, 1), roll(x, LANES - 1, 1))
    halves = roll(x, NZ, 1)
    row = row_of(x.shape) % SLICE
    next_pair = jnp.where(row == SLICE - 1, roll(halves, SLICE - 1, 0), roll(halves, ROWS - 1, 0))
    return jnp.where(lane_of(x.shape) < NZ, halves, next_pair)


def behind_of(direction, x):
    if direction == 3:
        first = lane_of(x.shape) % NZ == 0
        return jnp.where(first, roll(x, LANES - NZ + 1, 1), roll(x, 1, 1))
    halves = roll(x, NZ, 1)
    row = row_of(x.shape) % SLICE
    last_pair = jnp.where(row == 0, roll(halves, ROWS - SLICE + 1, 0), roll(halves, 1, 0))
    return jnp.where(lane_of(x.shape) < NZ, last_pair, halves)


def both_spins(half):
    return [jnp.concatenate(part, axis=0) for part in half]


def two_spins(real, imag):
    return [real[:3], real[3:]], [imag[:3], imag[3:]]


def to_bf16(x):
    return x.reshape(x.shape[0] // 2, 2 * ROWS, LANES).astype(jnp.bfloat16)


def to_f32(x):
    return x.astype(jnp.float32).reshape(2 * x.shape[0], ROWS, LANES)


def first_slice(real, imag):
    return jnp.where(row_of(real.shape) < SLICE, real, swap_slices(imag))


def last_slice(real, imag):
    return jnp.where(row_of(real.shape) < SLICE, swap_slices(real), imag)


def kernel(
    gauge_hbm, clover_hbm, source_hbm, xi_hbm, eta_hbm, momentum_hbm,
    solution_hbm, updated_hbm,
    gauge, clover_low, source, xi, eta, momentum,
    links, clover, psi, total, updated, t_ahead_local, t_behind_local,
    t_minus, t_plus, x_minus, x_plus,
    t_ahead, t_behind, x_ahead, x_behind,
    rim_t, rim_x, rim_t_ahead, rim_x_ahead,
    load_sem, store_sem, send_sem, recv_sem, rim_send_sem, rim_recv_sem,
):
    n_t, n_x = lax.axis_size("ta"), lax.axis_size("xyz")
    my_t, my_x = lax.axis_index("ta"), lax.axis_index("xyz")
    t_next, t_last = {"ta": lax.rem(my_t + 1, n_t)}, {"ta": lax.rem(my_t + n_t - 1, n_t)}
    x_next, x_last = {"xyz": lax.rem(my_x + 1, n_x)}, {"xyz": lax.rem(my_x + n_x - 1, n_x)}

    barrier = pltpu.get_barrier_semaphore()
    for device in (t_next, t_last, x_next, x_last):
        pl.semaphore_signal(barrier, inc=1, device_id=device, device_id_type=pl.DeviceIdType.MESH)

    loads = [
        pltpu.make_async_copy(src, dst, load_sem.at[i])
        for i, (src, dst) in enumerate([
            (source_hbm, source), (clover_hbm, clover_low), (gauge_hbm, gauge),
            (xi_hbm, xi), (eta_hbm, eta), (momentum_hbm, momentum),
        ])
    ]
    for load in loads:
        load.start()

    def remote(src, dst, send, recv, device):
        return pltpu.make_async_remote_copy(
            src_ref=src, dst_ref=dst, send_sem=send, recv_sem=recv,
            device_id=device, device_id_type=pl.DeviceIdType.MESH,
        )

    def halo_copies(slot):
        return [
            remote(src.at[slot], dst.at[slot], send_sem.at[i, slot], recv_sem.at[i, slot], device)
            for i, (src, dst, device) in enumerate([
                (t_minus, t_ahead, t_last), (t_plus, t_behind, t_next),
                (x_minus, x_ahead, x_last), (x_plus, x_behind, x_next),
            ])
        ]

    def rim_copies():
        return [
            remote(rim_t, rim_t_ahead, rim_send_sem.at[0], rim_recv_sem.at[0], t_last),
            remote(rim_x, rim_x_ahead, rim_send_sem.at[1], rim_recv_sem.at[1], x_last),
        ]

    def clover_apply(vector):
        for chiral in range(2):
            out_real = out_imag = None
            for j in range(6):
                spin, colour = 2 * chiral + j // 3, j % 3
                vec_real = vector[0][spin][colour : colour + 1]
                vec_imag = vector[1][spin][colour : colour + 1]
                mat_real = clover[chiral, 0, :, j]
                mat_imag = clover[chiral, 1, :, j]
                part_real = mat_real * vec_real - mat_imag * vec_imag
                part_imag = mat_real * vec_imag + mat_imag * vec_real
                out_real = part_real if j == 0 else out_real + part_real
                out_imag = part_imag if j == 0 else out_imag + part_imag
            for s in range(2):
                psi[0, 2 * chiral + s] = out_real[3 * s : 3 * s + 3]
                psi[1, 2 * chiral + s] = out_imag[3 * s : 3 * s + 3]

    def send_halos(slot):
        copies = halo_copies(slot)
        real, imag = both_spins(project(0, -1, psi))
        t_minus[slot] = to_bf16(first_slice(real, imag))
        copies[0].start()
        t_ahead_local[0] = swap_slices(real)
        t_ahead_local[1] = swap_slices(imag)
        real, imag = both_spins(dagger_apply(links, 0, project(0, 1, psi)))
        t_plus[slot] = to_bf16(last_slice(real, imag))
        copies[1].start()
        t_behind_local[0] = swap_slices(real)
        t_behind_local[1] = swap_slices(imag)
        x_minus[slot] = to_bf16(jnp.concatenate(both_spins(project(1, -1, psi)), axis=0))
        copies[2].start()
        x_plus[slot] = to_bf16(
            jnp.concatenate(both_spins(dagger_apply(links, 1, project(1, 1, psi))), axis=0)
        )
        copies[3].start()

    def read_total(ref):
        return [[ref[part, s] for s in range(4)] for part in range(2)]

    def local_hops():
        result = read_total(source)
        for direction in (2, 3):
            half = both_spins(project(direction, -1, psi))
            half = two_spins(*[ahead_of(direction, part) for part in half])
            result = add_expanded(result, direction, -1, link_apply(links, direction, half))
            half = both_spins(dagger_apply(links, direction, project(direction, 1, psi)))
            half = two_spins(*[behind_of(direction, part) for part in half])
            result = add_expanded(result, direction, 1, half)
        for part in range(2):
            for s in range(4):
                total[part, s] = result[part][s]

    def receive_halos(slot):
        copies = halo_copies(slot)
        result = read_total(total)
        copies[2].wait_recv()
        half = to_f32(x_ahead[slot])
        result = add_expanded(result, 1, -1, link_apply(links, 1, two_spins(half[:6], half[6:])))
        copies[3].wait_recv()
        half = to_f32(x_behind[slot])
        result = add_expanded(result, 1, 1, two_spins(half[:6], half[6:]))
        copies[0].wait_recv()
        rim = to_f32(t_ahead[slot])
        first = row_of(rim.shape) < SLICE
        half = two_spins(
            jnp.where(first, t_ahead_local[0], swap_slices(rim)), jnp.where(first, t_ahead_local[1], rim)
        )
        result = add_expanded(result, 0, -1, link_apply(links, 0, half))
        copies[1].wait_recv()
        rim = to_f32(t_behind[slot])
        half = two_spins(
            jnp.where(first, rim, t_behind_local[0]), jnp.where(first, swap_slices(rim), t_behind_local[1])
        )
        return add_expanded(result, 0, 1, half)

    def send_rims():
        copies = rim_copies()
        for i, (sign, field) in enumerate([(1, xi), (-1, eta)]):
            real, imag = both_spins(project(0, sign, field))
            rim_t[i] = first_slice(real, imag)
            real, imag = both_spins(project(1, sign, field))
            rim_x[i, 0] = real
            rim_x[i, 1] = imag
        for copy in copies:
            copy.start()

    def half_ahead(direction, sign, field, index):
        if direction == 1:
            return two_spins(rim_x_ahead[index, 0], rim_x_ahead[index, 1])
        real, imag = both_spins(project(direction, sign, field))
        if direction == 0:
            rim = rim_t_ahead[index]
            first = row_of(rim.shape) < SLICE
            real = jnp.where(first, swap_slices(real), swap_slices(rim))
            imag = jnp.where(first, swap_slices(imag), rim)
            return two_spins(real, imag)
        return two_spins(ahead_of(direction, real), ahead_of(direction, imag))

    def force(direction):
        outer_real = outer_imag = None
        for sign, field, index, other in ((-1, eta, 1, xi), (1, xi, 0, eta)):
            left_real, left_imag = half_ahead(direction, sign, field, index)
            right_real, right_imag = project(direction, sign, other)
            for s in range(2):
                lr, li = left_real[s][:, None], left_imag[s][:, None]
                rr, ri = right_real[s][None], right_imag[s][None]
                part_real = lr * rr + li * ri
                part_imag = li * rr - lr * ri
                outer_real = part_real if outer_real is None else outer_real + part_real
                outer_imag = part_imag if outer_imag is None else outer_imag + part_imag
        force_real = force_imag = None
        for c in range(3):
            mr, mi = gauge[direction, 0, :, c][:, None], gauge[direction, 1, :, c][:, None]
            orr, oi = outer_real[c][None], outer_imag[c][None]
            part_real = mr * orr - mi * oi
            part_imag = mr * oi + mi * orr
            force_real = part_real if c == 0 else force_real + part_real
            force_imag = part_imag if c == 0 else force_imag + part_imag
        half_step = 0.5 * step_size
        trace = (force_imag[0, 0] + force_imag[1, 1] + force_imag[2, 2]) * (step_size / 3.0)
        for a in range(3):
            updated[direction, 0, a, a] = momentum[direction, 0, a, a]
            updated[direction, 1, a, a] = momentum[direction, 1, a, a] - (
                step_size * force_imag[a, a] - trace
            )
            for b in range(a):
                anti = half_step * (force_real[a, b] - force_real[b, a])
                updated[direction, 0, a, b] = momentum[direction, 0, a, b] - anti
                updated[direction, 0, b, a] = momentum[direction, 0, b, a] + anti
                sym = half_step * (force_imag[a, b] + force_imag[b, a])
                updated[direction, 1, a, b] = momentum[direction, 1, a, b] - sym
                updated[direction, 1, b, a] = momentum[direction, 1, b, a] - sym

    store_updated = pltpu.make_async_copy(updated, updated_hbm, store_sem.at[0])
    store_solution = pltpu.make_async_copy(psi, solution_hbm, store_sem.at[1])

    loads[1].wait()
    out_row = lax.broadcasted_iota(jnp.int32, (LANES, LANES), 0)
    in_row = lax.broadcasted_iota(jnp.int32, (LANES, LANES), 1)
    place = (out_row // ROWS) * ROWS + (out_row % SLICE) * 2 + (out_row % ROWS) // SLICE
    permute = jnp.where(in_row == place, 1.0, 0.0).astype(jnp.bfloat16)
    blocks = LANES // ROWS
    for group in range(clover_low.shape[0] // LANES):
        moved = jnp.dot(
            permute, clover_low[group * LANES : (group + 1) * LANES], preferred_element_type=jnp.float32
        ).reshape(blocks, ROWS, LANES)
        for i in range(blocks):
            entry = group * blocks + i
            clover[entry // 72, entry // 36 % 2, entry // 6 % 6, entry % 6] = moved[i]
    loads[0].wait()
    clover_apply(read_total(source))
    loads[2].wait()
    for direction in range(4):
        for part in range(2):
            links[direction, part] = hop_scale * gauge[direction, part]
    pl.semaphore_wait(barrier, 4)
    send_halos(0)
    loads[3].wait()
    loads[4].wait()
    send_rims()
    loads[5].wait()

    def iteration(k, carry):
        slot = lax.rem(k - 1, 2)
        local_hops()

        @pl.when(k == 2)
        def _():
            for copy in rim_copies():
                copy.wait()
            for direction in range(4):
                force(direction)
            store_updated.start()

        clover_apply(receive_halos(slot))

        @pl.when(k < ITERS)
        def _():
            send_halos(lax.rem(k, 2))

        for copy in halo_copies(slot):
            copy.wait_send()
        return carry

    lax.fori_loop(1, ITERS + 1, iteration, 0)
    store_solution.start()
    store_updated.wait()
    store_solution.wait()


def per_device(gauge, clover_inverse, source, xi, eta, momentum):
    field = (2, 4, 3, ROWS, LANES)
    matrices = (4, 2, 3, 3, ROWS, LANES)
    half = (2, 3, 2 * ROWS, LANES)
    full = (2, 6, 2 * ROWS, LANES)
    chunks = LANES * SLICE // LANES
    low = clover_inverse.reshape(2, 2, 6, 6, 2, chunks, LANES)
    low = jnp.swapaxes(low, 4, 5).reshape(2 * 2 * 6 * 6 * chunks * 2, LANES)
    f32, bf16 = jnp.float32, jnp.bfloat16
    anywhere = pl.BlockSpec(memory_space=pl.ANY)
    solved, updated = pl.pallas_call(
        kernel,
        out_shape=(jax.ShapeDtypeStruct(field, f32), jax.ShapeDtypeStruct(matrices, f32)),
        in_specs=[anywhere] * 6,
        out_specs=(anywhere, anywhere),
        scratch_shapes=[
            pltpu.VMEM(matrices, f32),
            pltpu.VMEM(low.shape, bf16),
            pltpu.VMEM(field, f32),
            pltpu.VMEM(field, f32),
            pltpu.VMEM(field, f32),
            pltpu.VMEM(matrices, f32),
            pltpu.VMEM(matrices, f32),
            pltpu.VMEM((2, 2, 6, 6, ROWS, LANES), f32),
            pltpu.VMEM(field, f32),
            pltpu.VMEM(field, f32),
            pltpu.VMEM(matrices, f32),
            pltpu.VMEM((2, 6, ROWS, LANES), f32),
            pltpu.VMEM((2, 6, ROWS, LANES), f32),
            pltpu.VMEM(half, bf16),
            pltpu.VMEM(half, bf16),
            pltpu.VMEM(full, bf16),
            pltpu.VMEM(full, bf16),
            pltpu.VMEM(half, bf16),
            pltpu.VMEM(half, bf16),
            pltpu.VMEM(full, bf16),
            pltpu.VMEM(full, bf16),
            pltpu.VMEM((2, 6, ROWS, LANES), f32),
            pltpu.VMEM((2, 2, 6, ROWS, LANES), f32),
            pltpu.VMEM((2, 6, ROWS, LANES), f32),
            pltpu.VMEM((2, 2, 6, ROWS, LANES), f32),
            pltpu.SemaphoreType.DMA((6,)),
            pltpu.SemaphoreType.DMA((2,)),
            pltpu.SemaphoreType.DMA((4, 2)),
            pltpu.SemaphoreType.DMA((4, 2)),
            pltpu.SemaphoreType.DMA((2,)),
            pltpu.SemaphoreType.DMA((2,)),
        ],
        compiler_params=pltpu.CompilerParams(collective_id=0, has_side_effects=True),
        name="solve",
    )(
        gauge.reshape(matrices), low, source.reshape(field), xi.reshape(field),
        eta.reshape(field), momentum.reshape(matrices),
    )
    return solved.reshape(source.shape), updated.reshape(momentum.shape)


def solution(mesh):
    spinors = P(None, None, None, "ta", "xyz", None, None)
    matrices = P(None, None, None, None, "ta", "xyz", None, None)
    return jax.shard_map(
        per_device,
        mesh=mesh,
        in_specs=(matrices, matrices, spinors, spinors, spinors, matrices),
        out_specs=(spinors, matrices),
        check_vma=False,
    )
```

profile of v0, /device:TPU:1, one launch (start us, length us, event | category | flops | bytes accessed | tf_op | source)
XLA Modules:
  0.0 48.4 jit_solution(16651498275588761032)
XLA Ops:
  0.6 44.3 %solve.1 = (f32[2,4,3,8,128]{4,3,2,1,0:T(8,128)}, f32[4,2,3,3,8,128]{5,4,3,2,1,0:T(8,128)}) custom-call(f32[4,2,3,3,8,128]{5,4,3,2,1,0:T(8,128)} %bitcast.13, bf16[1152,128]{1,0:T(8,128)(2,1)} %bitcast.14, f32[2,4,3,8,128]{4,3,2,1,0:T(8,128)} %bitcast.16, f32[2,4,3,8,128]{4,3,2,1,0:T(8,128)} %bitcast.17, f32[2,4,3,8,128]{4,3,2,1,0:T(8,128)} %bitcast.18, ...), custom_call_target="tpu_custom_call" | custom-call | tf_op jit(solution)/shard_map/solve/pallas_call | solution.py:400
  44.9 1.5 %copy.13 = f32[2,4,3,2,1,1,512]{6,5,4,3,2,1,0:T(1,128)} copy(f32[2,4,3,2,1,1,512]{6,5,4,3,2,1,0:T(1,128)} %bitcast.19) | data formatting | bytes 196608
  46.5 1.9 %copy.14 = f32[4,2,3,3,2,1,1,512]{7,6,5,4,3,2,1,0:T(1,128)} copy(f32[4,2,3,3,2,1,1,512]{7,6,5,4,3,2,1,0:T(1,128)} %bitcast.12) | data formatting | bytes 589824
where the time goes:
time: 48.9 us; the launch traced here: 48.4 us
  Pallas kernels  44.3 us (91%)
  local copies, waits for them, and re-layouts  3.42 us (7%)
  between operations  0.64 us (1%)
    pallas_call x1, Pallas kernels, per_device(): pl.pallas_call(kernel, out_shape=(jax.ShapeDtypeStruct(field, f32), jax.S...  44.3 us
    unnamed x2, local copies, waits for them, and re-layouts  3.42 us

commit v1 on v0

--- a/solution.py
+++ b/solution.py
@@ -149,13 +149,13 @@
 
 def kernel(
     gauge_hbm, clover_hbm, source_hbm, xi_hbm, eta_hbm, momentum_hbm,
-    solution_hbm, updated_hbm,
+    psi, updated,
     gauge, clover_low, source, xi, eta, momentum,
-    links, clover, psi, total, updated, t_ahead_local, t_behind_local,
+    links, clover, total, t_ahead_local, t_behind_local,
     t_minus, t_plus, x_minus, x_plus,
     t_ahead, t_behind, x_ahead, x_behind,
     rim_t, rim_x, rim_t_ahead, rim_x_ahead,
-    load_sem, store_sem, send_sem, recv_sem, rim_send_sem, rim_recv_sem,
+    load_sem, send_sem, recv_sem, rim_send_sem, rim_recv_sem,
 ):
     n_t, n_x = lax.axis_size("ta"), lax.axis_size("xyz")
     my_t, my_x = lax.axis_index("ta"), lax.axis_index("xyz")
@@ -330,9 +330,6 @@
                 updated[direction, 1, a, b] = momentum[direction, 1, a, b] - sym
                 updated[direction, 1, b, a] = momentum[direction, 1, b, a] - sym
 
-    store_updated = pltpu.make_async_copy(updated, updated_hbm, store_sem.at[0])
-    store_solution = pltpu.make_async_copy(psi, solution_hbm, store_sem.at[1])
-
     loads[1].wait()
     out_row = lax.broadcasted_iota(jnp.int32, (LANES, LANES), 0)
     in_row = lax.broadcasted_iota(jnp.int32, (LANES, LANES), 1)
@@ -369,7 +366,6 @@
                 copy.wait()
             for direction in range(4):
                 force(direction)
-            store_updated.start()
 
         clover_apply(receive_halos(slot))
 
@@ -382,9 +378,17 @@
         return carry
 
     lax.fori_loop(1, ITERS + 1, iteration, 0)
-    store_solution.start()
-    store_updated.wait()
-    store_solution.wait()
+
+
+def publish(solved, updated, solved_out, updated_out, sem):
+    copies = [
+        pltpu.make_async_copy(solved, solved_out, sem.at[0]),
+        pltpu.make_async_copy(updated, updated_out, sem.at[1]),
+    ]
+    for copy in copies:
+        copy.start()
+    for copy in copies:
+        copy.wait()
 
 
 def per_device(gauge, clover_inverse, source, xi, eta, momentum):
@@ -397,11 +401,13 @@
     low = jnp.swapaxes(low, 4, 5).reshape(2 * 2 * 6 * 6 * chunks * 2, LANES)
     f32, bf16 = jnp.float32, jnp.bfloat16
     anywhere = pl.BlockSpec(memory_space=pl.ANY)
+    in_hbm = pl.BlockSpec(memory_space=pltpu.HBM)
+    on_chip = pl.BlockSpec(memory_space=pltpu.VMEM)
     solved, updated = pl.pallas_call(
         kernel,
-        out_shape=(jax.ShapeDtypeStruct(field, f32), jax.ShapeDtypeStruct(matrices, f32)),
+        out_shape=(pltpu.VMEM(field, f32), pltpu.VMEM(matrices, f32)),
         in_specs=[anywhere] * 6,
-        out_specs=(anywhere, anywhere),
+        out_specs=(on_chip, on_chip),
         scratch_shapes=[
             pltpu.VMEM(matrices, f32),
             pltpu.VMEM(low.shape, bf16),
@@ -412,8 +418,6 @@
             pltpu.VMEM(matrices, f32),
             pltpu.VMEM((2, 2, 6, 6, ROWS, LANES), f32),
             pltpu.VMEM(field, f32),
-            pltpu.VMEM(field, f32),
-            pltpu.VMEM(matrices, f32),
             pltpu.VMEM((2, 6, ROWS, LANES), f32),
             pltpu.VMEM((2, 6, ROWS, LANES), f32),
             pltpu.VMEM(half, bf16),
@@ -429,7 +433,6 @@
             pltpu.VMEM((2, 6, ROWS, LANES), f32),
             pltpu.VMEM((2, 2, 6, ROWS, LANES), f32),
             pltpu.SemaphoreType.DMA((6,)),
-            pltpu.SemaphoreType.DMA((2,)),
             pltpu.SemaphoreType.DMA((4, 2)),
             pltpu.SemaphoreType.DMA((4, 2)),
             pltpu.SemaphoreType.DMA((2,)),
@@ -441,6 +444,15 @@
         gauge.reshape(matrices), low, source.reshape(field), xi.reshape(field),
         eta.reshape(field), momentum.reshape(matrices),
     )
+    solved, updated = pl.pallas_call(
+        publish,
+        out_shape=(jax.ShapeDtypeStruct(field, f32), jax.ShapeDtypeStruct(matrices, f32)),
+        in_specs=[on_chip] * 2,
+        out_specs=(in_hbm, in_hbm),
+        scratch_shapes=[pltpu.SemaphoreType.DMA((2,))],
+        compiler_params=pltpu.CompilerParams(vmem_limit_bytes=1 << 20),
+        name="publish",
+    )(solved, updated)
     return solved.reshape(source.shape), updated.reshape(momentum.shape)
 
 

time: 48.9 us -> 45.6 us (0.933)
  local copies, waits for them, and re-layouts: 3.42 us -> 0 us
    unnamed x2 -> x0, local copies, waits for them, and re-layouts: 3.42 us -> none
    pallas_call x1 -> x2, Pallas kernels: 44.3 us -> 44.4 us  [the longest x1 43.7 us: per_device(): pl.pallas_call(kernel, out_shape=(pltpu.VMEM(field, f32), pltpu.VMEM(matr...]
where the time goes in v1:
time: 45.6 us; the launch traced here: 45.1 us
  Pallas kernels  44.4 us (97%)
  between operations  0.64 us (1%)
    pallas_call x1, Pallas kernels, per_device(): pl.pallas_call(kernel, out_shape=(pltpu.VMEM(field, f32), pltpu.VMEM(matr...  43.7 us

profile of v1, /device:TPU:1, one launch (start us, length us, event | category | flops | bytes accessed | tf_op | source)
XLA Modules:
  0.0 45.1 jit_solution(17682257947641862360)
XLA Ops:
  0.6 43.7 %solve.1 = (f32[2,4,3,8,128]{4,3,2,1,0:T(8,128)S(1)}, f32[4,2,3,3,8,128]{5,4,3,2,1,0:T(8,128)S(1)}) custom-call(f32[4,2,3,3,8,128]{5,4,3,2,1,0:T(8,128)} %bitcast.12, bf16[1152,128]{1,0:T(8,128)(2,1)} %bitcast.13, f32[2,4,3,8,128]{4,3,2,1,0:T(8,128)} %bitcast.15, f32[2,4,3,8,128]{4,3,2,1,0:T(8,128)} %bitcast.16, f32[2,4,3,8,128]{4,3,2,1,0:T(8,128)} %bitcast.17, ...), custom_call_target="tpu_custom_call" | custom-call | tf_op jit(solution)/shard_map/solve/pallas_call | solution.py:406
  44.3 0.8 %publish.1 = (f32[2,4,3,8,128]{4,3,2,1,0:T(8,128)}, f32[4,2,3,3,8,128]{5,4,3,2,1,0:T(8,128)}) custom-call(f32[2,4,3,8,128]{4,3,2,1,0:T(8,128)S(1)} %get-tuple-element.6.solved, f32[4,2,3,3,8,128]{5,4,3,2,1,0:T(8,128)S(1)} %get-tuple-element.7.updated), custom_call_target="tpu_custom_call" | custom-call | tf_op jit(solution)/shard_map/publish/pallas_call | solution.py:447

commit v2 on v1

--- a/solution.py
+++ b/solution.py
@@ -16,6 +16,10 @@
 ROWS = 8
 LANES = 128
 SLICE = 4
+
+SWITCH = 4
+RIMS_AT = 4
+FORCE_AT = 6
 
 
 def combine(base, sign, term):
@@ -147,6 +151,15 @@
     return jnp.where(row_of(real.shape) < SLICE, swap_slices(real), imag)
 
 
+def spread(first, last):
+    top = row_of(first.shape) < SLICE
+    return jnp.where(top, first, swap_slices(last)), jnp.where(top, swap_slices(first), last)
+
+
+def masked(rows, part):
+    return jnp.where(rows, part, 0.0)
+
+
 def kernel(
     gauge_hbm, clover_hbm, source_hbm, xi_hbm, eta_hbm, momentum_hbm,
     psi, updated,
@@ -155,16 +168,19 @@
     t_minus, t_plus, x_minus, x_plus,
     t_ahead, t_behind, x_ahead, x_behind,
     rim_t, rim_x, rim_t_ahead, rim_x_ahead,
-    load_sem, send_sem, recv_sem, rim_send_sem, rim_recv_sem,
+    rest, rest_in, corner, corner_in, bulk_clover, bulk_clover_in, bulk_links, bulk_links_in,
+    clover_rim, links_rim, psi_rim, halo,
+    load_sem, send_sem, recv_sem, once_send_sem, once_recv_sem, ready,
 ):
     n_t, n_x = lax.axis_size("ta"), lax.axis_size("xyz")
     my_t, my_x = lax.axis_index("ta"), lax.axis_index("xyz")
     t_next, t_last = {"ta": lax.rem(my_t + 1, n_t)}, {"ta": lax.rem(my_t + n_t - 1, n_t)}
     x_next, x_last = {"xyz": lax.rem(my_x + 1, n_x)}, {"xyz": lax.rem(my_x + n_x - 1, n_x)}
+    mesh_id = pl.DeviceIdType.MESH
 
     barrier = pltpu.get_barrier_semaphore()
     for device in (t_next, t_last, x_next, x_last):
-        pl.semaphore_signal(barrier, inc=1, device_id=device, device_id_type=pl.DeviceIdType.MESH)
+        pl.semaphore_signal(barrier, inc=1, device_id=device, device_id_type=mesh_id)
 
     loads = [
         pltpu.make_async_copy(src, dst, load_sem.at[i])
@@ -179,64 +195,116 @@
     def remote(src, dst, send, recv, device):
         return pltpu.make_async_remote_copy(
             src_ref=src, dst_ref=dst, send_sem=send, recv_sem=recv,
-            device_id=device, device_id_type=pl.DeviceIdType.MESH,
+            device_id=device, device_id_type=mesh_id,
         )
 
-    def halo_copies(slot):
+    def slot_copy(index, slot, src, dst, device):
+        return remote(src, dst, send_sem.at[index, slot], recv_sem.at[index, slot], device)
+
+    def t_copies(slot):
         return [
-            remote(src.at[slot], dst.at[slot], send_sem.at[i, slot], recv_sem.at[i, slot], device)
-            for i, (src, dst, device) in enumerate([
-                (t_minus, t_ahead, t_last), (t_plus, t_behind, t_next),
-                (x_minus, x_ahead, x_last), (x_plus, x_behind, x_next),
-            ])
+            slot_copy(0, slot, t_minus.at[slot], t_ahead.at[slot], t_last),
+            slot_copy(1, slot, t_plus.at[slot], t_behind.at[slot], t_next),
         ]
 
+    def x_copies(slot):
+        return [
+            slot_copy(2, slot, x_minus.at[slot], x_ahead.at[slot], x_last),
+            slot_copy(3, slot, x_plus.at[slot], x_behind.at[slot], x_next),
+        ]
+
+    def rest_copies(slot):
+        return [
+            slot_copy(4 + i, slot, rest.at[slot, i], rest_in.at[slot, i], device)
+            for i, device in enumerate((t_last, t_next))
+        ]
+
+    def corner_copies(slot):
+        devices = [{**t, **x} for t in (t_last, t_next) for x in (x_last, x_next)]
+        return [
+            slot_copy(6 + i, slot, corner.at[slot, i], corner_in.at[slot, i], device)
+            for i, device in enumerate(devices)
+        ]
+
+    def once_copy(index, src, dst, device):
+        return remote(src, dst, once_send_sem.at[index], once_recv_sem.at[index], device)
+
     def rim_copies():
-        return [
-            remote(rim_t, rim_t_ahead, rim_send_sem.at[0], rim_recv_sem.at[0], t_last),
-            remote(rim_x, rim_x_ahead, rim_send_sem.at[1], rim_recv_sem.at[1], x_last),
-        ]
-
-    def clover_apply(vector):
+        return [once_copy(0, rim_t, rim_t_ahead, t_last), once_copy(1, rim_x, rim_x_ahead, x_last)]
+
+    def bulk_copies():
+        copies = []
+        for i, device in enumerate((t_last, t_next)):
+            copies.append(once_copy(2 + i, bulk_clover.at[i], bulk_clover_in.at[i], device))
+            copies.append(once_copy(4 + i, bulk_links.at[i], bulk_links_in.at[i], device))
+        return copies
+
+    def clover_apply(blocks, vector, out):
         for chiral in range(2):
             out_real = out_imag = None
             for j in range(6):
                 spin, colour = 2 * chiral + j // 3, j % 3
                 vec_real = vector[0][spin][colour : colour + 1]
                 vec_imag = vector[1][spin][colour : colour + 1]
-                mat_real = clover[chiral, 0, :, j]
-                mat_imag = clover[chiral, 1, :, j]
+                mat_real = blocks[chiral, 0, :, j]
+                mat_imag = blocks[chiral, 1, :, j]
                 part_real = mat_real * vec_real - mat_imag * vec_imag
                 part_imag = mat_real * vec_imag + mat_imag * vec_real
                 out_real = part_real if j == 0 else out_real + part_real
                 out_imag = part_imag if j == 0 else out_imag + part_imag
             for s in range(2):
-                psi[0, 2 * chiral + s] = out_real[3 * s : 3 * s + 3]
-                psi[1, 2 * chiral + s] = out_imag[3 * s : 3 * s + 3]
-
-    def send_halos(slot):
-        copies = halo_copies(slot)
+                out[0, 2 * chiral + s] = out_real[3 * s : 3 * s + 3]
+                out[1, 2 * chiral + s] = out_imag[3 * s : 3 * s + 3]
+
+    def send_halos(j):
+        kept = lax.rem(j, 2)
         real, imag = both_spins(project(0, -1, psi))
-        t_minus[slot] = to_bf16(first_slice(real, imag))
+        t_ahead_local[kept, 0] = swap_slices(real)
+        t_ahead_local[kept, 1] = swap_slices(imag)
+        real, imag = both_spins(dagger_apply(links, 0, project(0, 1, psi)))
+        t_behind_local[kept, 0] = swap_slices(real)
+        t_behind_local[kept, 1] = swap_slices(imag)
+
+        @pl.when(j < SWITCH - 1)
+        def _():
+            copies = t_copies(j)
+            top = row_of((6, ROWS, LANES)) < SLICE
+            t_minus[j] = to_bf16(
+                jnp.where(top, swap_slices(t_ahead_local[kept, 0]), t_ahead_local[kept, 1])
+            )
+            copies[0].start()
+            t_plus[j] = to_bf16(
+                jnp.where(top, t_behind_local[kept, 0], swap_slices(t_behind_local[kept, 1]))
+            )
+            copies[1].start()
+
+        copies = x_copies(j)
+        x_minus[j] = to_bf16(jnp.concatenate(both_spins(project(1, -1, psi)), axis=0))
         copies[0].start()
-        t_ahead_local[0] = swap_slices(real)
-        t_ahead_local[1] = swap_slices(imag)
-        real, imag = both_spins(dagger_apply(links, 0, project(0, 1, psi)))
-        t_plus[slot] = to_bf16(last_slice(real, imag))
-        copies[1].start()
-        t_behind_local[0] = swap_slices(real)
-        t_behind_local[1] = swap_slices(imag)
-        x_minus[slot] = to_bf16(jnp.concatenate(both_spins(project(1, -1, psi)), axis=0))
-        copies[2].start()
-        x_plus[slot] = to_bf16(
+        x_plus[j] = to_bf16(
             jnp.concatenate(both_spins(dagger_apply(links, 1, project(1, 1, psi))), axis=0)
         )
-        copies[3].start()
+        copies[1].start()
+
+        @pl.when((j >= SWITCH - 2) & (j < ITERS - 1))
+        def _():
+            copies = corner_copies(j)
+            for i, sent in enumerate((x_minus, x_plus)):
+                value = to_f32(sent[j])
+                corner[j, i] = to_bf16(first_slice(value[:6], value[6:]))
+                copies[i].start()
+                corner[j, 2 + i] = to_bf16(last_slice(value[:6], value[6:]))
+                copies[2 + i].start()
 
     def read_total(ref):
         return [[ref[part, s] for s in range(4)] for part in range(2)]
 
-    def local_hops():
+    def write_total(ref, result):
+        for part in range(2):
+            for s in range(4):
+                ref[part, s] = result[part][s]
+
+    def local_hops(kept):
         result = read_total(source)
         for direction in (2, 3):
             half = both_spins(project(direction, -1, psi))
@@ -245,32 +313,97 @@
             half = both_spins(dagger_apply(links, direction, project(direction, 1, psi)))
             half = two_spins(*[behind_of(direction, part) for part in half])
             result = add_expanded(result, direction, 1, half)
-        for part in range(2):
-            for s in range(4):
-                total[part, s] = result[part][s]
-
-    def receive_halos(slot):
-        copies = halo_copies(slot)
+        top = row_of((6, ROWS, LANES)) < SLICE
+        half = two_spins(*[masked(top, t_ahead_local[kept, part]) for part in range(2)])
+        result = add_expanded(result, 0, -1, link_apply(links, 0, half))
+        half = two_spins(*[masked(~top, t_behind_local[kept, part]) for part in range(2)])
+        write_total(total, add_expanded(result, 0, 1, half))
+
+    def send_rest(k):
+        copies = rest_copies(k)
+        real, imag = [jnp.concatenate(part, axis=0) for part in read_total(total)]
+        rest[k, 0] = to_bf16(first_slice(real, imag))
+        copies[0].start()
+        rest[k, 1] = to_bf16(last_slice(real, imag))
+        copies[1].start()
+
+    def receive_bulk():
+        for copy in bulk_copies():
+            copy.wait_recv()
+        for chiral in range(2):
+            real, imag = spread(to_f32(bulk_clover_in[0, chiral]), to_f32(bulk_clover_in[1, chiral]))
+            clover_rim[chiral, 0] = real.reshape(6, 6, ROWS, LANES)
+            clover_rim[chiral, 1] = imag.reshape(6, 6, ROWS, LANES)
+        real, imag = spread(to_f32(bulk_links_in[0]), to_f32(bulk_links_in[1]))
+        for direction in range(2):
+            links_rim[direction, 0] = real[9 * direction : 9 * direction + 9].reshape(3, 3, ROWS, LANES)
+            links_rim[direction, 1] = imag[9 * direction : 9 * direction + 9].reshape(3, 3, ROWS, LANES)
+
+    def receive_t(j):
+        copies = t_copies(j)
+        top = row_of((6, ROWS, LANES)) < SLICE
+        copies[0].wait_recv()
+        rim = to_f32(t_ahead[j])
+        halo[0, 0] = masked(~top, swap_slices(rim))
+        halo[0, 1] = masked(~top, rim)
+        copies[1].wait_recv()
+        rim = to_f32(t_behind[j])
+        halo[1, 0] = masked(top, rim)
+        halo[1, 1] = masked(top, swap_slices(rim))
+
+    def iterate_rim(k):
+        kept = lax.rem(k - 1, 2)
+        top = row_of((6, ROWS, LANES)) < SLICE
+        zero = jnp.zeros((3, ROWS, LANES), jnp.float32)
+        result = [[zero] * 4, [zero] * 4]
+        half = two_spins(*[masked(top, t_behind_local[kept, part]) for part in range(2)])
+        result = add_expanded(result, 0, 1, half)
+        half = two_spins(*[masked(~top, t_ahead_local[kept, part]) for part in range(2)])
+        result = add_expanded(result, 0, -1, link_apply(links_rim, 0, half))
+        for copy in rest_copies(k):
+            copy.wait_recv()
+        parts = spread(to_f32(rest_in[k, 0]), to_f32(rest_in[k, 1]))
+        result = [
+            [result[part][s] + parts[part][3 * s : 3 * s + 3] for s in range(4)] for part in range(2)
+        ]
+        for copy in corner_copies(k - 1):
+            copy.wait_recv()
+        half = two_spins(*spread(to_f32(corner_in[k - 1, 0]), to_f32(corner_in[k - 1, 2])))
+        result = add_expanded(result, 1, -1, link_apply(links_rim, 1, half))
+        half = two_spins(*spread(to_f32(corner_in[k - 1, 1]), to_f32(corner_in[k - 1, 3])))
+        clover_apply(clover_rim, add_expanded(result, 1, 1, half), psi_rim)
+        for part, value in enumerate(both_spins(project(0, -1, psi_rim))):
+            halo[0, part] = masked(~top, swap_slices(value))
+        for part, value in enumerate(both_spins(dagger_apply(links_rim, 0, project(0, 1, psi_rim)))):
+            halo[1, part] = masked(top, swap_slices(value))
+
+    def with_halos(slot):
+        copies = x_copies(slot)
         result = read_total(total)
-        copies[2].wait_recv()
+        half = two_spins(halo[0, 0], halo[0, 1])
+        result = add_expanded(result, 0, -1, link_apply(links, 0, half))
+        result = add_expanded(result, 0, 1, two_spins(halo[1, 0], halo[1, 1]))
+        copies[0].wait_recv()
         half = to_f32(x_ahead[slot])
         result = add_expanded(result, 1, -1, link_apply(links, 1, two_spins(half[:6], half[6:])))
-        copies[3].wait_recv()
+        copies[1].wait_recv()
         half = to_f32(x_behind[slot])
-        result = add_expanded(result, 1, 1, two_spins(half[:6], half[6:]))
-        copies[0].wait_recv()
-        rim = to_f32(t_ahead[slot])
-        first = row_of(rim.shape) < SLICE
-        half = two_spins(
-            jnp.where(first, t_ahead_local[0], swap_slices(rim)), jnp.where(first, t_ahead_local[1], rim)
-        )
-        result = add_expanded(result, 0, -1, link_apply(links, 0, half))
-        copies[1].wait_recv()
-        rim = to_f32(t_behind[slot])
-        half = two_spins(
-            jnp.where(first, rim, t_behind_local[0]), jnp.where(first, swap_slices(rim), t_behind_local[1])
-        )
-        return add_expanded(result, 0, 1, half)
+        return add_expanded(result, 1, 1, two_spins(half[:6], half[6:]))
+
+    def send_bulk():
+        for chiral in range(2):
+            real = clover[chiral, 0].reshape(36, ROWS, LANES)
+            imag = clover[chiral, 1].reshape(36, ROWS, LANES)
+            bulk_clover[0, chiral] = to_bf16(first_slice(real, imag))
+            bulk_clover[1, chiral] = to_bf16(last_slice(real, imag))
+        real, imag = [
+            jnp.concatenate([links[d, part].reshape(9, ROWS, LANES) for d in range(2)], axis=0)
+            for part in range(2)
+        ]
+        bulk_links[0] = to_bf16(first_slice(real, imag))
+        bulk_links[1] = to_bf16(last_slice(real, imag))
+        for copy in bulk_copies():
+            copy.start()
 
     def send_rims():
         copies = rim_copies()
@@ -344,40 +477,67 @@
             entry = group * blocks + i
             clover[entry // 72, entry // 36 % 2, entry // 6 % 6, entry % 6] = moved[i]
     loads[0].wait()
-    clover_apply(read_total(source))
+    clover_apply(clover, read_total(source), psi)
     loads[2].wait()
     for direction in range(4):
         for part in range(2):
             links[direction, part] = hop_scale * gauge[direction, part]
     pl.semaphore_wait(barrier, 4)
     send_halos(0)
-    loads[3].wait()
-    loads[4].wait()
-    send_rims()
-    loads[5].wait()
+    for device in (x_next, x_last):
+        pl.semaphore_signal(ready, inc=1, device_id=device, device_id_type=mesh_id)
+    send_bulk()
+    for load in loads[3:]:
+        load.wait()
+    pl.semaphore_wait(ready, 2)
 
     def iteration(k, carry):
-        slot = lax.rem(k - 1, 2)
-        local_hops()
-
-        @pl.when(k == 2)
+        local_hops(lax.rem(k - 1, 2))
+
+        @pl.when((k >= SWITCH - 1) & (k < ITERS))
+        def _():
+            send_rest(k)
+
+        @pl.when(k == RIMS_AT)
+        def _():
+            send_rims()
+
+        @pl.when(k == FORCE_AT)
         def _():
             for copy in rim_copies():
                 copy.wait()
             for direction in range(4):
                 force(direction)
 
-        clover_apply(receive_halos(slot))
+        @pl.when(k < SWITCH)
+        def _():
+            receive_t(k - 1)
+
+        @pl.when(k == SWITCH)
+        def _():
+            receive_bulk()
+
+        @pl.when(k >= SWITCH)
+        def _():
+            iterate_rim(k - 1)
+
+        clover_apply(clover, with_halos(k - 1), psi)
 
         @pl.when(k < ITERS)
         def _():
-            send_halos(lax.rem(k, 2))
-
-        for copy in halo_copies(slot):
-            copy.wait_send()
+            send_halos(k)
+
         return carry
 
     lax.fori_loop(1, ITERS + 1, iteration, 0)
+    sent = bulk_copies()
+    for j in range(ITERS):
+        sent += x_copies(j)
+        sent += t_copies(j) if j < SWITCH - 1 else []
+        sent += corner_copies(j) if SWITCH - 2 <= j < ITERS - 1 else []
+        sent += rest_copies(j) if j >= SWITCH - 1 else []
+    for copy in sent:
+        copy.wait_send()
 
 
 def publish(solved, updated, solved_out, updated_out, sem):
@@ -394,8 +554,8 @@
 def per_device(gauge, clover_inverse, source, xi, eta, momentum):
     field = (2, 4, 3, ROWS, LANES)
     matrices = (4, 2, 3, 3, ROWS, LANES)
-    half = (2, 3, 2 * ROWS, LANES)
-    full = (2, 6, 2 * ROWS, LANES)
+    half = (3, 2 * ROWS, LANES)
+    full = (6, 2 * ROWS, LANES)
     chunks = LANES * SLICE // LANES
     low = clover_inverse.reshape(2, 2, 6, 6, 2, chunks, LANES)
     low = jnp.swapaxes(low, 4, 5).reshape(2 * 2 * 6 * 6 * chunks * 2, LANES)
@@ -418,25 +578,38 @@
             pltpu.VMEM(matrices, f32),
             pltpu.VMEM((2, 2, 6, 6, ROWS, LANES), f32),
             pltpu.VMEM(field, f32),
-            pltpu.VMEM((2, 6, ROWS, LANES), f32),
-            pltpu.VMEM((2, 6, ROWS, LANES), f32),
-            pltpu.VMEM(half, bf16),
-            pltpu.VMEM(half, bf16),
-            pltpu.VMEM(full, bf16),
-            pltpu.VMEM(full, bf16),
-            pltpu.VMEM(half, bf16),
-            pltpu.VMEM(half, bf16),
-            pltpu.VMEM(full, bf16),
-            pltpu.VMEM(full, bf16),
+            pltpu.VMEM((2, 2, 6, ROWS, LANES), f32),
+            pltpu.VMEM((2, 2, 6, ROWS, LANES), f32),
+            pltpu.VMEM((SWITCH - 1, *half), bf16),
+            pltpu.VMEM((SWITCH - 1, *half), bf16),
+            pltpu.VMEM((ITERS, *full), bf16),
+            pltpu.VMEM((ITERS, *full), bf16),
+            pltpu.VMEM((SWITCH - 1, *half), bf16),
+            pltpu.VMEM((SWITCH - 1, *half), bf16),
+            pltpu.VMEM((ITERS, *full), bf16),
+            pltpu.VMEM((ITERS, *full), bf16),
             pltpu.VMEM((2, 6, ROWS, LANES), f32),
             pltpu.VMEM((2, 2, 6, ROWS, LANES), f32),
             pltpu.VMEM((2, 6, ROWS, LANES), f32),
             pltpu.VMEM((2, 2, 6, ROWS, LANES), f32),
+            pltpu.VMEM((ITERS, 2, *full), bf16),
+            pltpu.VMEM((ITERS, 2, *full), bf16),
+            pltpu.VMEM((ITERS, 4, *half), bf16),
+            pltpu.VMEM((ITERS, 4, *half), bf16),
+            pltpu.VMEM((2, 2, 18, 2 * ROWS, LANES), bf16),
+            pltpu.VMEM((2, 2, 18, 2 * ROWS, LANES), bf16),
+            pltpu.VMEM((2, 9, 2 * ROWS, LANES), bf16),
+            pltpu.VMEM((2, 9, 2 * ROWS, LANES), bf16),
+            pltpu.VMEM((2, 2, 6, 6, ROWS, LANES), f32),
+            pltpu.VMEM((2, 2, 3, 3, ROWS, LANES), f32),
+            pltpu.VMEM(field, f32),
+            pltpu.VMEM((2, 2, 6, ROWS, LANES), f32),
             pltpu.SemaphoreType.DMA((6,)),
-            pltpu.SemaphoreType.DMA((4, 2)),
-            pltpu.SemaphoreType.DMA((4, 2)),
-            pltpu.SemaphoreType.DMA((2,)),
-            pltpu.SemaphoreType.DMA((2,)),
+            pltpu.SemaphoreType.DMA((10, ITERS)),
+            pltpu.SemaphoreType.DMA((10, ITERS)),
+            pltpu.SemaphoreType.DMA((6,)),
+            pltpu.SemaphoreType.DMA((6,)),
+            pltpu.SemaphoreType.REGULAR,
         ],
         compiler_params=pltpu.CompilerParams(collective_id=0, has_side_effects=True),
         name="solve",

time: 45.6 us -> 43 us (0.943)
  Pallas kernels: 44.4 us -> 42.2 us
    pallas_call x1, Pallas kernels: 43.7 us -> 41.5 us  [per_device(): pl.pallas_call(kernel, out_shape=(pltpu.VMEM(field, f32), pltpu.VMEM(matr...]
where the time goes in v2:
time: 43 us; the launch traced here: 42.9 us
  Pallas kernels  42.2 us (98%)
  between operations  0.64 us (1%)
    pallas_call x1, Pallas kernels, per_device(): pl.pallas_call(kernel, out_shape=(pltpu.VMEM(field, f32), pltpu.VMEM(matr...  41.5 us

profile of v2, /device:TPU:1, one launch (start us, length us, event | category | flops | bytes accessed | tf_op | source)
XLA Modules:
  0.0 42.9 jit_solution(5606768944443538682)
XLA Ops:
  0.6 41.5 %solve.1 = (f32[2,4,3,8,128]{4,3,2,1,0:T(8,128)S(1)}, f32[4,2,3,3,8,128]{5,4,3,2,1,0:T(8,128)S(1)}) custom-call(f32[4,2,3,3,8,128]{5,4,3,2,1,0:T(8,128)} %bitcast.12, bf16[1152,128]{1,0:T(8,128)(2,1)} %bitcast.13, f32[2,4,3,8,128]{4,3,2,1,0:T(8,128)} %bitcast.15, f32[2,4,3,8,128]{4,3,2,1,0:T(8,128)} %bitcast.16, f32[2,4,3,8,128]{4,3,2,1,0:T(8,128)} %bitcast.17, ...), custom_call_target="tpu_custom_call" | custom-call | tf_op jit(solution)/shard_map/solve/pallas_call | solution.py:566
  42.1 0.8 %publish.1 = (f32[2,4,3,8,128]{4,3,2,1,0:T(8,128)}, f32[4,2,3,3,8,128]{5,4,3,2,1,0:T(8,128)}) custom-call(f32[2,4,3,8,128]{4,3,2,1,0:T(8,128)S(1)} %get-tuple-element.6.solved, f32[4,2,3,3,8,128]{5,4,3,2,1,0:T(8,128)S(1)} %get-tuple-element.7.updated), custom_call_target="tpu_custom_call" | custom-call | tf_op jit(solution)/shard_map/publish/pallas_call | solution.py:620

commit v3 on v2

--- a/solution.py
+++ b/solution.py
@@ -17,7 +17,7 @@
 LANES = 128
 SLICE = 4
 
-SWITCH = 4
+SWITCH = 3
 RIMS_AT = 4
 FORCE_AT = 6
 
@@ -235,7 +235,9 @@
     def bulk_copies():
         copies = []
         for i, device in enumerate((t_last, t_next)):
-            copies.append(once_copy(2 + i, bulk_clover.at[i], bulk_clover_in.at[i], device))
+            copies.append(once_copy(2 + i, bulk_clover.at[i, 0], bulk_clover_in.at[i, 0], device))
+        for i, device in enumerate((t_last, t_next)):
+            copies.append(once_copy(6 + i, bulk_clover.at[i, 1], bulk_clover_in.at[i, 1], device))
             copies.append(once_copy(4 + i, bulk_links.at[i], bulk_links_in.at[i], device))
         return copies
 
@@ -256,7 +258,16 @@
                 out[0, 2 * chiral + s] = out_real[3 * s : 3 * s + 3]
                 out[1, 2 * chiral + s] = out_imag[3 * s : 3 * s + 3]
 
-    def send_halos(j):
+    def send_x(j):
+        copies = x_copies(j)
+        x_minus[j] = to_bf16(jnp.concatenate(both_spins(project(1, -1, psi)), axis=0))
+        copies[0].start()
+        x_plus[j] = to_bf16(
+            jnp.concatenate(both_spins(dagger_apply(links, 1, project(1, 1, psi))), axis=0)
+        )
+        copies[1].start()
+
+    def keep_t(j):
         kept = lax.rem(j, 2)
         real, imag = both_spins(project(0, -1, psi))
         t_ahead_local[kept, 0] = swap_slices(real)
@@ -265,36 +276,28 @@
         t_behind_local[kept, 0] = swap_slices(real)
         t_behind_local[kept, 1] = swap_slices(imag)
 
-        @pl.when(j < SWITCH - 1)
-        def _():
-            copies = t_copies(j)
-            top = row_of((6, ROWS, LANES)) < SLICE
-            t_minus[j] = to_bf16(
-                jnp.where(top, swap_slices(t_ahead_local[kept, 0]), t_ahead_local[kept, 1])
-            )
-            copies[0].start()
-            t_plus[j] = to_bf16(
-                jnp.where(top, t_behind_local[kept, 0], swap_slices(t_behind_local[kept, 1]))
-            )
-            copies[1].start()
-
-        copies = x_copies(j)
-        x_minus[j] = to_bf16(jnp.concatenate(both_spins(project(1, -1, psi)), axis=0))
+    def send_t(j):
+        kept = lax.rem(j, 2)
+        copies = t_copies(j)
+        real, imag = both_spins(project(0, -1, psi))
+        t_minus[j] = to_bf16(first_slice(real, imag))
         copies[0].start()
-        x_plus[j] = to_bf16(
-            jnp.concatenate(both_spins(dagger_apply(links, 1, project(1, 1, psi))), axis=0)
-        )
+        t_ahead_local[kept, 0] = swap_slices(real)
+        t_ahead_local[kept, 1] = swap_slices(imag)
+        real, imag = both_spins(dagger_apply(links, 0, project(0, 1, psi)))
+        t_plus[j] = to_bf16(last_slice(real, imag))
         copies[1].start()
-
-        @pl.when((j >= SWITCH - 2) & (j < ITERS - 1))
-        def _():
-            copies = corner_copies(j)
-            for i, sent in enumerate((x_minus, x_plus)):
-                value = to_f32(sent[j])
-                corner[j, i] = to_bf16(first_slice(value[:6], value[6:]))
-                copies[i].start()
-                corner[j, 2 + i] = to_bf16(last_slice(value[:6], value[6:]))
-                copies[2 + i].start()
+        t_behind_local[kept, 0] = swap_slices(real)
+        t_behind_local[kept, 1] = swap_slices(imag)
+
+    def send_corners(j):
+        copies = corner_copies(j)
+        for i, sent in enumerate((x_minus, x_plus)):
+            value = to_f32(sent[j])
+            corner[j, i] = to_bf16(first_slice(value[:6], value[6:]))
+            copies[i].start()
+            corner[j, 2 + i] = to_bf16(last_slice(value[:6], value[6:]))
+            copies[2 + i].start()
 
     def read_total(ref):
         return [[ref[part, s] for s in range(4)] for part in range(2)]
@@ -390,7 +393,7 @@
         half = to_f32(x_behind[slot])
         return add_expanded(result, 1, 1, two_spins(half[:6], half[6:]))
 
-    def send_bulk():
+    def pack_bulk():
         for chiral in range(2):
             real = clover[chiral, 0].reshape(36, ROWS, LANES)
             imag = clover[chiral, 1].reshape(36, ROWS, LANES)
@@ -402,8 +405,6 @@
         ]
         bulk_links[0] = to_bf16(first_slice(real, imag))
         bulk_links[1] = to_bf16(last_slice(real, imag))
-        for copy in bulk_copies():
-            copy.start()
 
     def send_rims():
         copies = rim_copies()
@@ -483,10 +484,13 @@
         for part in range(2):
             links[direction, part] = hop_scale * gauge[direction, part]
     pl.semaphore_wait(barrier, 4)
-    send_halos(0)
+    send_t(0)
+    send_x(0)
     for device in (x_next, x_last):
         pl.semaphore_signal(ready, inc=1, device_id=device, device_id_type=mesh_id)
-    send_bulk()
+    pack_bulk()
+    for copy in bulk_copies()[:2]:
+        copy.start()
     for load in loads[3:]:
         load.wait()
     pl.semaphore_wait(ready, 2)
@@ -523,9 +527,24 @@
 
         clover_apply(clover, with_halos(k - 1), psi)
 
-        @pl.when(k < ITERS)
-        def _():
-            send_halos(k)
+        @pl.when(k < SWITCH - 1)
+        def _():
+            send_t(k)
+            send_x(k)
+
+        @pl.when(k == 1)
+        def _():
+            for copy in bulk_copies()[2:]:
+                copy.start()
+
+        @pl.when((k >= SWITCH - 1) & (k < ITERS))
+        def _():
+            send_x(k)
+            keep_t(k)
+
+        @pl.when((k >= SWITCH - 2) & (k < ITERS - 1))
+        def _():
+            send_corners(k)
 
         return carry
 
@@ -607,8 +626,8 @@
             pltpu.SemaphoreType.DMA((6,)),
             pltpu.SemaphoreType.DMA((10, ITERS)),
             pltpu.SemaphoreType.DMA((10, ITERS)),
-            pltpu.SemaphoreType.DMA((6,)),
-            pltpu.SemaphoreType.DMA((6,)),
+            pltpu.SemaphoreType.DMA((8,)),
+            pltpu.SemaphoreType.DMA((8,)),
             pltpu.SemaphoreType.REGULAR,
         ],
         compiler_params=pltpu.CompilerParams(collective_id=0, has_side_effects=True),

time: 43 us -> 42.2 us (0.981)
  Pallas kernels: 42.2 us -> 41.5 us
    pallas_call x1, Pallas kernels: 41.5 us -> 40.7 us  [per_device(): pl.pallas_call(kernel, out_shape=(pltpu.VMEM(field, f32), pltpu.VMEM(matr...]
where the time goes in v3:
time: 42.2 us; the launch traced here: 42.1 us
  Pallas kernels  41.5 us (98%)
  between operations  0.64 us (2%)
    pallas_call x1, Pallas kernels, per_device(): pl.pallas_call(kernel, out_shape=(pltpu.VMEM(field, f32), pltpu.VMEM(matr...  40.7 us

profile of v3, /device:TPU:1, one launch (start us, length us, event | category | flops | bytes accessed | tf_op | source)
XLA Modules:
  0.0 42.1 jit_solution(331667838367491425)
XLA Ops:
  0.6 40.7 %solve.1 = (f32[2,4,3,8,128]{4,3,2,1,0:T(8,128)S(1)}, f32[4,2,3,3,8,128]{5,4,3,2,1,0:T(8,128)S(1)}) custom-call(f32[4,2,3,3,8,128]{5,4,3,2,1,0:T(8,128)} %bitcast.12, bf16[1152,128]{1,0:T(8,128)(2,1)} %bitcast.13, f32[2,4,3,8,128]{4,3,2,1,0:T(8,128)} %bitcast.15, f32[2,4,3,8,128]{4,3,2,1,0:T(8,128)} %bitcast.16, f32[2,4,3,8,128]{4,3,2,1,0:T(8,128)} %bitcast.17, ...), custom_call_target="tpu_custom_call" | custom-call | tf_op jit(solution)/shard_map/solve/pallas_call | solution.py:585
  41.4 0.8 %publish.1 = (f32[2,4,3,8,128]{4,3,2,1,0:T(8,128)}, f32[4,2,3,3,8,128]{5,4,3,2,1,0:T(8,128)}) custom-call(f32[2,4,3,8,128]{4,3,2,1,0:T(8,128)S(1)} %get-tuple-element.6.solved, f32[4,2,3,3,8,128]{5,4,3,2,1,0:T(8,128)S(1)} %get-tuple-element.7.updated), custom_call_target="tpu_custom_call" | custom-call | tf_op jit(solution)/shard_map/publish/pallas_call | solution.py:639

commit v4 on v3

--- a/solution.py
+++ b/solution.py
@@ -287,6 +287,23 @@
         real, imag = both_spins(dagger_apply(links, 0, project(0, 1, psi)))
         t_plus[j] = to_bf16(last_slice(real, imag))
         copies[1].start()
+        t_behind_local[kept, 0] = swap_slices(real)
+        t_behind_local[kept, 1] = swap_slices(imag)
+
+    def pack_x(j):
+        x_minus[j] = to_bf16(jnp.concatenate(both_spins(project(1, -1, psi)), axis=0))
+        x_plus[j] = to_bf16(
+            jnp.concatenate(both_spins(dagger_apply(links, 1, project(1, 1, psi))), axis=0)
+        )
+
+    def pack_t(j):
+        kept = lax.rem(j, 2)
+        real, imag = both_spins(project(0, -1, psi))
+        t_minus[j] = to_bf16(first_slice(real, imag))
+        t_ahead_local[kept, 0] = swap_slices(real)
+        t_ahead_local[kept, 1] = swap_slices(imag)
+        real, imag = both_spins(dagger_apply(links, 0, project(0, 1, psi)))
+        t_plus[j] = to_bf16(last_slice(real, imag))
         t_behind_local[kept, 0] = swap_slices(real)
         t_behind_local[kept, 1] = swap_slices(imag)
 
@@ -380,12 +397,12 @@
         for part, value in enumerate(both_spins(dagger_apply(links_rim, 0, project(0, 1, psi_rim)))):
             halo[1, part] = masked(top, swap_slices(value))
 
-    def with_halos(slot):
+    def with_t(result):
+        result = add_expanded(result, 0, -1, link_apply(links, 0, two_spins(halo[0, 0], halo[0, 1])))
+        return add_expanded(result, 0, 1, two_spins(halo[1, 0], halo[1, 1]))
+
+    def with_x(result, slot):
         copies = x_copies(slot)
-        result = read_total(total)
-        half = two_spins(halo[0, 0], halo[0, 1])
-        result = add_expanded(result, 0, -1, link_apply(links, 0, half))
-        result = add_expanded(result, 0, 1, two_spins(halo[1, 0], halo[1, 1]))
         copies[0].wait_recv()
         half = to_f32(x_ahead[slot])
         result = add_expanded(result, 1, -1, link_apply(links, 1, two_spins(half[:6], half[6:])))
@@ -483,9 +500,11 @@
     for direction in range(4):
         for part in range(2):
             links[direction, part] = hop_scale * gauge[direction, part]
+    pack_t(0)
+    pack_x(0)
     pl.semaphore_wait(barrier, 4)
-    send_t(0)
-    send_x(0)
+    for copy in t_copies(0) + x_copies(0):
+        copy.start()
     for device in (x_next, x_last):
         pl.semaphore_signal(ready, inc=1, device_id=device, device_id_type=mesh_id)
     pack_bulk()
@@ -495,60 +514,63 @@
         load.wait()
     pl.semaphore_wait(ready, 2)
 
-    def iteration(k, carry):
-        local_hops(lax.rem(k - 1, 2))
-
-        @pl.when((k >= SWITCH - 1) & (k < ITERS))
-        def _():
+    def near_iteration(k):
+        local_hops((k - 1) % 2)
+        if k >= SWITCH - 1:
             send_rest(k)
-
-        @pl.when(k == RIMS_AT)
-        def _():
-            send_rims()
-
-        @pl.when(k == FORCE_AT)
-        def _():
-            for copy in rim_copies():
-                copy.wait()
-            for direction in range(4):
-                force(direction)
-
-        @pl.when(k < SWITCH)
-        def _():
-            receive_t(k - 1)
-
-        @pl.when(k == SWITCH)
-        def _():
-            receive_bulk()
-
-        @pl.when(k >= SWITCH)
-        def _():
-            iterate_rim(k - 1)
-
-        clover_apply(clover, with_halos(k - 1), psi)
-
-        @pl.when(k < SWITCH - 1)
-        def _():
+        write_total(total, with_x(read_total(total), k - 1))
+        receive_t(k - 1)
+        clover_apply(clover, with_t(read_total(total)), psi)
+        if k < SWITCH - 1:
             send_t(k)
             send_x(k)
-
-        @pl.when(k == 1)
-        def _():
+        else:
+            send_x(k)
+            keep_t(k)
+        if k == 1:
             for copy in bulk_copies()[2:]:
                 copy.start()
-
-        @pl.when((k >= SWITCH - 1) & (k < ITERS))
-        def _():
+        if k >= SWITCH - 2:
+            send_corners(k)
+
+    def far_iteration(k, last=False):
+        local_hops(lax.rem(k - 1, 2))
+        if not last:
+            send_rest(k)
+
+            @pl.when(k == RIMS_AT)
+            def _():
+                send_rims()
+
+            @pl.when(k == FORCE_AT)
+            def _():
+                for copy in rim_copies():
+                    copy.wait()
+                for direction in range(4):
+                    force(direction)
+
+            @pl.when(k == SWITCH)
+            def _():
+                receive_bulk()
+
+        iterate_rim(k - 1)
+        clover_apply(clover, with_x(with_t(read_total(total)), k - 1), psi)
+        if not last:
             send_x(k)
             keep_t(k)
 
-        @pl.when((k >= SWITCH - 2) & (k < ITERS - 1))
-        def _():
-            send_corners(k)
-
+            @pl.when(k < ITERS - 1)
+            def _():
+                send_corners(k)
+
+    def looped(k, carry):
+        far_iteration(k)
         return carry
 
-    lax.fori_loop(1, ITERS + 1, iteration, 0)
+    for k in range(1, SWITCH):
+        near_iteration(k)
+    lax.fori_loop(SWITCH, ITERS, looped, 0)
+    far_iteration(ITERS, last=True)
     sent = bulk_copies()
     for j in range(ITERS):
         sent += x_copies(j)

time: 42.2 us -> 41.8 us (level)
    pallas_call x1, Pallas kernels: 40.7 us -> 40.3 us  [per_device(): pl.pallas_call(kernel, out_shape=(pltpu.VMEM(field, f32), pltpu.VMEM(matr...]
where the time goes in v4:
time: 41.8 us; the launch traced here: 41.7 us
  Pallas kernels  41.1 us (98%)
  between operations  0.64 us (2%)
    pallas_call x1, Pallas kernels, per_device(): pl.pallas_call(kernel, out_shape=(pltpu.VMEM(field, f32), pltpu.VMEM(matr...  40.3 us

profile of v4, /device:TPU:1, one launch (start us, length us, event | category | flops | bytes accessed | tf_op | source)
XLA Modules:
  0.0 41.7 jit_solution(7635921316457808521)
XLA Ops:
  0.6 40.3 %solve.1 = (f32[2,4,3,8,128]{4,3,2,1,0:T(8,128)S(1)}, f32[4,2,3,3,8,128]{5,4,3,2,1,0:T(8,128)S(1)}) custom-call(f32[4,2,3,3,8,128]{5,4,3,2,1,0:T(8,128)} %bitcast.12, bf16[1152,128]{1,0:T(8,128)(2,1)} %bitcast.13, f32[2,4,3,8,128]{4,3,2,1,0:T(8,128)} %bitcast.15, f32[2,4,3,8,128]{4,3,2,1,0:T(8,128)} %bitcast.16, f32[2,4,3,8,128]{4,3,2,1,0:T(8,128)} %bitcast.17, ...), custom_call_target="tpu_custom_call" | custom-call | tf_op jit(solution)/shard_map/solve/pallas_call | solution.py:607
  40.9 0.8 %publish.1 = (f32[2,4,3,8,128]{4,3,2,1,0:T(8,128)}, f32[4,2,3,3,8,128]{5,4,3,2,1,0:T(8,128)}) custom-call(f32[2,4,3,8,128]{4,3,2,1,0:T(8,128)S(1)} %get-tuple-element.6.solved, f32[4,2,3,3,8,128]{5,4,3,2,1,0:T(8,128)S(1)} %get-tuple-element.7.updated), custom_call_target="tpu_custom_call" | custom-call | tf_op jit(solution)/shard_map/publish/pallas_call | solution.py:661

commit v5 on v4

--- a/solution.py
+++ b/solution.py
@@ -259,13 +259,9 @@
                 out[1, 2 * chiral + s] = out_imag[3 * s : 3 * s + 3]
 
     def send_x(j):
-        copies = x_copies(j)
-        x_minus[j] = to_bf16(jnp.concatenate(both_spins(project(1, -1, psi)), axis=0))
-        copies[0].start()
-        x_plus[j] = to_bf16(
-            jnp.concatenate(both_spins(dagger_apply(links, 1, project(1, 1, psi))), axis=0)
-        )
-        copies[1].start()
+        pack_x(j)
+        for copy in x_copies(j):
+            copy.start()
 
     def keep_t(j):
         kept = lax.rem(j, 2)
@@ -404,9 +400,9 @@
     def with_x(result, slot):
         copies = x_copies(slot)
         copies[0].wait_recv()
+        copies[1].wait_recv()
         half = to_f32(x_ahead[slot])
         result = add_expanded(result, 1, -1, link_apply(links, 1, two_spins(half[:6], half[6:])))
-        copies[1].wait_recv()
         half = to_f32(x_behind[slot])
         return add_expanded(result, 1, 1, two_spins(half[:6], half[6:]))
 

time: 41.8 us -> 41.8 us (level)
  no operation moved by 1% of the time
where the time goes in v5:
time: 41.8 us; the launch traced here: 41.7 us
  Pallas kernels  41 us (98%)
  between operations  0.64 us (2%)
    pallas_call x1, Pallas kernels, per_device(): pl.pallas_call(kernel, out_shape=(pltpu.VMEM(field, f32), pltpu.VMEM(matr...  40.3 us

profile of v5, /device:TPU:1, one launch (start us, length us, event | category | flops | bytes accessed | tf_op | source)
XLA Modules:
  0.0 41.7 jit_solution(10755598932549040390)
XLA Ops:
  0.6 40.3 %solve.1 = (f32[2,4,3,8,128]{4,3,2,1,0:T(8,128)S(1)}, f32[4,2,3,3,8,128]{5,4,3,2,1,0:T(8,128)S(1)}) custom-call(f32[4,2,3,3,8,128]{5,4,3,2,1,0:T(8,128)} %bitcast.12, bf16[1152,128]{1,0:T(8,128)(2,1)} %bitcast.13, f32[2,4,3,8,128]{4,3,2,1,0:T(8,128)} %bitcast.15, f32[2,4,3,8,128]{4,3,2,1,0:T(8,128)} %bitcast.16, f32[2,4,3,8,128]{4,3,2,1,0:T(8,128)} %bitcast.17, ...), custom_call_target="tpu_custom_call" | custom-call | tf_op jit(solution)/shard_map/solve/pallas_call | solution.py:603
  40.9 0.8 %publish.1 = (f32[2,4,3,8,128]{4,3,2,1,0:T(8,128)}, f32[4,2,3,3,8,128]{5,4,3,2,1,0:T(8,128)}) custom-call(f32[2,4,3,8,128]{4,3,2,1,0:T(8,128)S(1)} %get-tuple-element.6.solved, f32[4,2,3,3,8,128]{5,4,3,2,1,0:T(8,128)S(1)} %get-tuple-element.7.updated), custom_call_target="tpu_custom_call" | custom-call | tf_op jit(solution)/shard_map/publish/pallas_call | solution.py:657
